TPU v7x, 256 devices: a whole 4x4x8 slice. The times are simulated.
256 devices in a mesh: dp: 4 (over y), space: 64 (over x, z, core).
Axes of the slice: x: 4, y: 4, z: 8, core: 2. Of those that a mesh axis runs over, the one named last changes fastest.
Arguments:
- volume: bfloat16 [4, 128, 4, 64, 128], P('dp', 'space'), may hold values from -30 to 30
- weights_one: bfloat16 [3, 3, 3, 128, 256], replicated, may hold values from -0.109375 to 0.109375
- gain_one: float32 [256], replicated, may hold values from 0.1 to 1.9
- shift_one: float32 [256], replicated, may hold values from -3 to 3
- weights_two: bfloat16 [3, 3, 3, 8, 256], P(None, None, None, None, 'space'), may hold values from -0.4375 to 0.4375
- gain_two: float32 [256], P('space'), may hold values from 0.1 to 1.9
- shift_two: float32 [256], P('space'), may hold values from -3 to 3
- upstream: bfloat16 [4, 256, 64, 2, 32], P('dp', 'space'), may hold values from -6 to 6
Outputs:
- result: bfloat16 [4, 256, 64, 2, 32], P('dp', 'space')
- grad_weights_one: float32 [3, 3, 3, 128, 256], P(None, None, None, None, 'space')
- grad_weights_two: float32 [3, 3, 3, 8, 256], P(None, None, None, None, 'space')
All inputs are finite; a program needn't handle non-finite values.
Results may differ from a plain program's by a relative error of at most 0.0057.
Values may be sent and summed in bfloat16 or wider, within the bound.
A program may use at most 64 MiB of HBM per device.

v0:
```python
import math
import jax
import jax.numpy as jnp
from jax import lax
from jax.sharding import PartitionSpec as P

EPS = 1e-05
LAST = ("NDHWC", "DHWIO", "NDHWC")
FIRST = ("NCDHW", "DHWIO", "NCDHW")


def from_behind(value, axis, steps):
    count = lax.axis_size(axis)
    leading, last = (max(0, -steps), min(count, count - steps))
    return lax.ppermute(value, axis, [(source, source + steps) for source in range(leading, last)])


def combined_all(part, axis, combine):
    gathered = jax.tree.map(lambda a: lax.all_gather(a, axis), part)

    def take(source):
        return jax.tree.map(lambda a: lax.dynamic_index_in_dim(a, source, 0, False), gathered)

    return lax.fori_loop(
        1, lax.axis_size(axis), lambda source, state: combine(state, take(source)), take(0)
    )


def welford(left, right):
    count_a, mean_a, spread_a = left
    count_b, mean_b, spread_b = right
    merged = count_a + count_b
    delta = mean_b - mean_a
    return (
        merged,
        mean_a + delta * (count_b / merged),
        spread_a + spread_b + delta * delta * (count_a * count_b / merged),
    )


def group_filter(inputs, grads):
    return lax.conv_general_dilated(
        inputs,
        grads,
        (1, 1, 1),
        ((1, 1), (1, 1), (1, 1)),
        dimension_numbers=("CNDHW", "IODHW", "DHWNC"),
        preferred_element_type=jnp.float32,
    )


def per_device(
    volume, weights_one, gain_one, shift_one, weights_two, gain_two, shift_two, upstream
):
    planes = lax.axis_size("space")
    below = from_behind(volume[:, 1:], "space", 1)
    stacked = jnp.concatenate([below, volume], axis=1)
    pre_one = lax.conv_general_dilated(
        stacked,
        weights_one,
        (2, 2, 2),
        ((0, 0), (1, 1), (1, 1)),
        dimension_numbers=LAST,
        preferred_element_type=jnp.float32,
    )
    lead = pre_one.shape[0]
    count = float(lax.axis_size("dp") * lead * planes * pre_one.shape[2] * pre_one.shape[3])
    axes_last = (0, 1, 2, 3)
    mean_one = lax.psum(jnp.sum(pre_one, axis=axes_last), ("dp", "space")) / count
    spread_one = lax.psum(jnp.sum(jnp.square(pre_one - mean_one), axis=axes_last), ("dp", "space"))
    var_one = spread_one / count
    inv_one = lax.rsqrt(var_one + EPS)
    norm_one = (pre_one - mean_one) * inv_one
    act_in = norm_one * gain_one + shift_one
    activated = jax.nn.silu(act_in).astype(jnp.bfloat16)
    act_first = jnp.transpose(activated, (0, 4, 1, 2, 3))
    own_width = weights_two.shape[4]
    group_width = weights_two.shape[3]
    window = max(own_width, group_width)
    replicas = window // own_width
    channels = act_first.shape[1]
    tail = act_first.shape[2:]
    parts = act_first.reshape((lead, channels // window, 1, window) + tail)
    copies = jnp.broadcast_to(parts, (lead, channels // window, replicas, window) + tail)
    outgoing = copies.reshape((lead, planes * window) + tail)
    inputs = lax.all_to_all(outgoing, "space", split_axis=1, concat_axis=2, tiled=True)
    groups_here = window // group_width
    per_group = own_width // groups_here
    padding_one = ((1, 1), (1, 1), (1, 1))
    pre_two = lax.conv_general_dilated(
        inputs,
        weights_two,
        (1, 1, 1),
        padding_one,
        dimension_numbers=FIRST,
        feature_group_count=groups_here,
        preferred_element_type=jnp.float32,
    )
    axes_first = (0, 2, 3, 4)
    local_mean_two = jnp.mean(pre_two, axis=axes_first, keepdims=True)
    local_spread_two = jnp.sum(jnp.square(pre_two - local_mean_two), axis=axes_first, keepdims=True)
    local_count_two = float(pre_two.size // pre_two.shape[1])
    merged_two, mean_two, spread_two = combined_all(
        (jnp.full((1, 1, 1, 1, 1), local_count_two, jnp.float32), local_mean_two, local_spread_two),
        "dp",
        welford,
    )
    inv_two = lax.rsqrt(spread_two / merged_two + EPS)
    norm_two = (pre_two - mean_two) * inv_two
    gain_col = gain_two.reshape((1, -1, 1, 1, 1))
    shift_col = shift_two.reshape((1, -1, 1, 1, 1))
    result = (norm_two * gain_col + shift_col).astype(jnp.bfloat16)
    grad_norm_two = upstream.astype(jnp.float32) * gain_col * (1.0 / math.sqrt(count))
    first_sum, second_sum = lax.psum(
        (
            jnp.sum(grad_norm_two, axis=axes_first, keepdims=True),
            jnp.sum(grad_norm_two * norm_two, axis=axes_first, keepdims=True),
        ),
        "dp",
    )
    grad_pre_two = (
        inv_two * (grad_norm_two - first_sum / count - norm_two * (second_sum / count))
    ).astype(jnp.bfloat16)
    grouped_inputs = inputs.reshape((lead, groups_here, group_width) + inputs.shape[2:])
    grouped_grads = grad_pre_two.reshape((lead, groups_here, per_group) + grad_pre_two.shape[2:])
    pieces = jax.vmap(group_filter, in_axes=(1, 1))(grouped_inputs, grouped_grads)
    local_two = jnp.transpose(pieces, (1, 2, 3, 4, 0, 5)).reshape((3, 3, 3, group_width, own_width))
    grad_weights_two = lax.psum(local_two, "dp")
    flipped = weights_two[::-1, ::-1, ::-1]
    turned = (
        flipped.reshape((3, 3, 3, group_width, groups_here, per_group))
        .transpose((0, 1, 2, 5, 4, 3))
        .reshape((3, 3, 3, per_group, window))
    )
    partial_grad = lax.conv_general_dilated(
        grad_pre_two,
        turned,
        (1, 1, 1),
        padding_one,
        dimension_numbers=FIRST,
        feature_group_count=groups_here,
        preferred_element_type=jnp.float32,
    )
    arrived = lax.all_to_all(partial_grad, "space", split_axis=2, concat_axis=1, tiled=True)
    grad_act = jnp.sum(
        arrived.reshape((lead, channels // window, replicas, window) + arrived.shape[2:]), axis=2
    ).reshape((lead, channels) + arrived.shape[2:])
    grad_last = jnp.transpose(grad_act, (0, 2, 3, 4, 1))
    sigma = jax.nn.sigmoid(act_in)
    grad_norm_one = grad_last * (sigma * (1.0 + act_in * (1.0 - sigma))) * gain_one
    third_sum, fourth_sum = lax.psum(
        (jnp.sum(grad_norm_one, axis=axes_last), jnp.sum(grad_norm_one * norm_one, axis=axes_last)),
        ("dp", "space"),
    )
    grad_pre_one = (
        inv_one * (grad_norm_one - third_sum / count - norm_one * (fourth_sum / count))
    ).astype(jnp.bfloat16)
    local_one = lax.conv_general_dilated(
        stacked,
        grad_pre_one,
        (1, 1, 1),
        ((0, 0), (1, 0), (1, 0)),
        rhs_dilation=(2, 2, 2),
        dimension_numbers=("CDHWN", "IDHWO", "DHWNC"),
        preferred_element_type=jnp.float32,
    )
    summed = lax.psum(local_one, "dp")
    grad_weights_one = lax.psum_scatter(summed, "space", scatter_dimension=4, tiled=True)
    return (result, grad_weights_one, grad_weights_two)


def solution(mesh):
    return jax.shard_map(
        per_device,
        mesh=mesh,
        in_specs=(
            P("dp", "space", None, None, None),
            P(),
            P(),
            P(),
            P(None, None, None, None, "space"),
            P("space"),
            P("space"),
            P("dp", "space", None, None, None),
        ),
        out_specs=(
            P("dp", "space", None, None, None),
            P(None, None, None, None, "space"),
            P(None, None, None, None, "space"),
        ),
        check_vma=False,
    )
```

profile of v0, /device:TPU:2, one launch (start us, length us, event | category | flops | bytes accessed | tf_op | source)
XLA Modules:
  0.0 559.2 jit_solution(1003987523249396105)
XLA Ops:
  7.2 1.0 slice.21
  8.3 1.9 collective-permute-start
  10.2 7.9 %collective-permute-done = bf16[1,1,4,64,128]{4,0,3,2,1:T(2,128)(2,1)S(1)} collective-permute-done((bf16[1,1,4,64,128]{4,0,3,2,1:T(2,128)(2,1)S(1)}, bf16[1,1,4,64,128]{4,0,3,2,1:T(2,128)(2,1)S(1)}, u32[]{:S(2)}, u32[]{:S(2)}) %collective-permute-start) | collective-permute-done | bytes 65568 | tf_op jit(solution)/shard_map/ppermute | solution.py:15
  18.1 0.1 constant_dynamic-update-slice_fusion.1
  18.2 1.1 constant_dynamic-update-slice_fusion
  19.4 0.7 copy-done.1
  20.2 0.2 copy.244
  20.5 0.4 select_reduce_fusion.3
  21.0 74.9 %psum.56 = f32[256]{0:T(256)S(1)} all-reduce(f32[256]{0:T(256)S(1)} %get-tuple-element.289), channel_id=1, replica_groups=mesh['dp'=4,'space'=64] {'dp','space'}, use_global_device_ids=true, to_apply=%region_1.0 | all-reduce | flops 256 | bytes 2048 | tf_op jit(solution)/shard_map/psum | solution.py:69
  95.9 74.4 %psum.57 = f32[256]{0:T(256)S(1)} all-reduce(f32[256]{0:T(256)S(1)} %select_reduce_fusion.2), channel_id=1, replica_groups=mesh['dp'=4,'space'=64] {'dp','space'}, use_global_device_ids=true, to_apply=%region_3.0 | all-reduce | flops 256 | bytes 2048 | tf_op jit(solution)/shard_map/psum | solution.py:70
  170.5 0.4 copy-done.9
  171.1 0.1 copy.203
  171.2 0.1 broadcast_in_dim.11
  171.3 0.8 reshape.180
  172.2 8.1 %all-to-all-start = ((bf16[64,2,256]{2,1,0:T(2,128)(2,1)}), bf16[64,2,256]{2,1,0:T(2,128)(2,1)S(1)}, u32[]{:S(2)}, u32[]{:S(2)}) async-start(bf16[64,2,256]{2,1,0:T(2,128)(2,1)} %reshape.180), calls=%async_computation | async-start | bytes 131072 | tf_op jit(solution)/shard_map/all_to_all | solution.py:86
  180.3 0.6 rev.3
  180.9 0.6 dynamic-slice
  182.2 0.8 dynamic-update-slice
  183.0 6.0 %all-to-all-done = bf16[64,2,256]{2,1,0:T(2,128)(2,1)S(1)} async-done(((bf16[64,2,256]{2,1,0:T(2,128)(2,1)}), bf16[64,2,256]{2,1,0:T(2,128)(2,1)S(1)}, u32[]{:S(2)}, u32[]{:S(2)}) %all-to-all-start) | async-done | bytes 65568 | tf_op jit(solution)/shard_map/all_to_all | solution.py:86
  189.1 0.2 reshape.181
  189.3 0.2 copy.245
  189.5 0.7 pad.2.clone
  190.2 2.1 copy.207
  192.3 0.2 slice.24
  192.5 5.6 fusion.8
  198.1 1.7 copy.208
  199.8 0.2 select_reduce_fusion.1
  200.1 0.2 select_reduce_fusion
  200.3 0.2 dynamic-update-slice.2
  200.5 8.6 %all-reduce.7 = (f32[4]{0:T(128)S(1)}, f32[16]{0:T(128)S(1)}, f32[16]{0:T(128)S(1)}) all-reduce(f32[4]{0:T(128)S(1)} %dynamic-update-slice, f32[16]{0:T(128)S(1)} %get-tuple-element.288, f32[16]{0:T(128)S(1)} %dynamic-update-slice.2), channel_id=1, replica_groups=mesh['dp'=4,'space'=64] {'dp'}, use_global_device_ids=true, to_apply=%add | all-reduce | flops 36 | bytes 288
  209.8 13.6 %while.19 = (s32[]{:T(128)}, f32[1,1,1,1,1]{4,3,2,1,0:T(1,128)}, f32[1,4,1,1,1]{1,4,3,2,0:T(1,128)S(1)}, f32[1,4,1,1,1]{1,4,3,2,0:T(1,128)S(1)}, f32[4,1,1,1,1,1...) while((s32[]{:T(128)}, f32[1,1,1,1,1]{4,3,2,1,0:T(1,128)}, ...), condition=%wide.region_7.8_spmd, body=%wide.region_6.7_spmd.sunk | while | flops 37 | bytes 303 | solution.py:24
  209.8 0.6 constant_dynamic-slice_fusion.5
  214.4 0.6 constant_dynamic-slice_fusion.5
  218.9 0.6 constant_dynamic-slice_fusion.5
  223.5 0.7 rsqrt_bitcast_fusion
  224.1 0.8 add_convert_fusion
  224.9 0.3 fusion.39
  225.2 9.4 %all-reduce.6 = (f32[1,4,1,1,1]{1,4,3,2,0:T(1,128)S(1)}, f32[1,4,1,1,1]{1,4,3,2,0:T(1,128)S(1)}) all-reduce(f32[1,4,1,1,1]{1,4,3,2,0:T(1,128)S(1)} %bitcast.177, f32[1,4,1,1,1]{1,4,3,2,0:T(1,128)S(1)} %bitcast.176), channel_id=1, replica_groups=mesh['dp'=4,'space'=64] {'dp'}, use_global_device_ids=true, to_apply=%region_11.12 | all-reduce | flops 8 | bytes 64 | tf_op jit(solution)/shard_map/psum | solution.py:114
  234.9 0.4 copy.218
  235.3 0.2 slice.28
  235.5 6.9 %convolution_select_fusion = f32[64,2,8,5,8]{4,2,3,1,0:T(8,128)} fusion(pred[8,5]{0,1:T(8,128)(4,1)S(1)} %copy-done.7, bf16[4,64,2,1,7,2]{4,0,5,2,1,3:T(4,128)(2,1)S(1)} %slice.28, bf16[4,64,2,1,8,5]{4,0,5,2,1,3:T(4,128)(2,1)S(1)} %copy.218, bf16[3,3,3,8,4]{3,4,2,1,0:T(4,128)(2,1)S(1)} %copy-done.6), kind=kOutput, calls=%fused_computation.19 | convolution fusion | flops 6049792 | bytes 220904 | tf_op jit(solution)/shard_map/conv_general_dilated | solution.py:135
  242.5 2.6 copy.219
  245.1 0.3 copy.220
  245.4 0.9 reshape.182
  246.4 5.5 all-to-all-start.1
  252.2 0.8 copy.241
  253.0 8.2 %all-to-all-done.1 = f32[64,1,512]{2,1,0:T(1,128)S(1)} async-done(((f32[64,1,512]{2,1,0:T(1,128)}), f32[64,1,512]{2,1,0:T(1,128)S(1)}, u32[]{:S(2)}, u32[]{:S(2)}) %all-to-all-start.1) | async-done | bytes 131104 | tf_op jit(solution)/shard_map/all_to_all | solution.py:144
  261.2 0.5 broadcast.186
  261.7 0.9 reduce.1
  262.7 0.2 reshape.183
  262.9 0.7 reduce_sum.87
  263.6 1.3 fusion.51
  264.9 73.3 %all-reduce.4 = (f32[256]{0:T(256)S(1)}, f32[256]{0:T(256)S(1)}) all-reduce(f32[256]{0:T(256)S(1)} %get-tuple-element.252, f32[256]{0:T(256)S(1)} %get-tuple-element.251), channel_id=1, replica_groups=mesh['dp'=4,'space'=64] {'dp','space'}, use_global_device_ids=true, to_apply=%region_16.17 | all-reduce | flops 512 | bytes 4096 | tf_op jit(solution)/shard_map/psum | solution.py:151
  338.4 0.8 fusion.31
  339.4 2.8 fusion.53
  342.3 0.6 copy-done.13
  342.9 0.6 dynamic-slice.3
  344.1 3.5 copy.231
  347.7 0.6 copy.232
  348.3 3.4 copy.230
  351.7 29.6 %fusion.54 = f32[3,3,3,8,4]{3,4,2,1,0:T(4,128)S(1)} fusion(bf16[1,8,64,2,32]{1,0,4,3,2:T(2,128)(2,1)} %copy.230, bf16[1,4,64,2,32]{1,0,4,3,2:T(2,128)(2,1)} %copy.231), kind=kOutput, calls=%fused_computation.97 | convolution fusion | flops 4572160 | bytes 101760 | tf_op jit(solution)/shard_map/vmap()/conv_general_dilated | solution.py:42
  381.3 151.0 %all-reduce.10.cloned.1.call-done = f32[3,3,3,128,256]{3,4,2,1,0:T(8,128)} async-done(((f32[3,3,3,128,256]{3,4,2,1,0:T(8,128)}), f32[3,3,3,128,256]{3,4,2,1,0:T(8,128)}) %all-reduce.10.cloned.1.call-update) | async-done | bytes 3538960
  532.3 0.9 constant_dynamic-slice_fusion.3
  533.3 18.7 %all-reduce.5 = (f32[3,3,3,128,4]{3,4,2,1,0:T(4,128)}, f32[3,3,3,8,4]{3,4,2,1,0:T(4,128)}) all-reduce(f32[3,3,3,128,4]{3,4,2,1,0:T(4,128)S(1)} %constant_dynamic-slice_fusion.3, f32[3,3,3,8,4]{3,4,2,1,0:T(4,128)S(1)} %fusion.54), channel_id=1, replica_groups=mesh['dp'=4,'space'=64] {'dp'}, use_global_device_ids=true, to_apply=%region_17.18 | all-reduce | flops 14688 | bytes 117504 | tf_op jit(solution)/shard_map/psum | solution.py:167
  (75 shorter events, 2.1 us)
Async XLA Ops:
  7.2 13.3 %copy-start = (bf16[3,3,3,128,256]{4,3,2,1,0:T(8,128)(2,1)S(1)}, bf16[3,3,3,128,256]{4,3,2,1,0:T(8,128)(2,1)}, u32[]{:S(2)}) copy-start(bf16[3,3,3,128,256]{4,3,2,1,0:T(8,128)(2,1)} %param.11) | copy-start | bytes 5308420
  7.2 13.3 %copy-start.7 = (pred[8,5]{0,1:T(8,128)(4,1)S(1)}, pred[8,5]{0,1:T(8,128)(4,1)}, u32[]{:S(2)}) copy-start(pred[8,5]{0,1:T(8,128)(4,1)} %constant.99) | copy-start | bytes 124
  8.3 9.8 %collective-permute-start = (bf16[1,1,4,64,128]{4,0,3,2,1:T(2,128)(2,1)S(1)}, bf16[1,1,4,64,128]{4,0,3,2,1:T(2,128)(2,1)S(1)}, u32[]{:S(2)}, u32[]{:S(2)}) collective-permute-start(bf16[1,1,4,64,128]{4,0,3,2,1:T(2,128)(2,1)S(1)} %copy.254), channel_id=1, source_target_pairs={{0,1},{1,2},{2,3},{3,4},{4,5},{5,6},{6,7},{7,8},{8,9},{9,10},{10,1... | collective-permute-start | bytes 196616 | tf_op jit(solution)/shard_map/ppermute | solution.py:15
  19.4 0.7 copy-start.1
  20.1 150.2 %copy-start.8 = (f32[256]{0:T(256)S(1)}, f32[256]{0:T(256)}, u32[]{:S(2)}) copy-start(f32[256]{0:T(256)} %param.12) | copy-start | bytes 3076
  20.1 150.2 %copy-start.11 = (f32[256]{0:T(256)S(1)}, f32[256]{0:T(256)}, u32[]{:S(2)}) copy-start(f32[256]{0:T(256)} %param.13) | copy-start | bytes 3076
  20.5 159.8 %copy-start.5 = (bf16[3,3,3,8,4]{3,4,2,1,0:T(4,128)(2,1)S(1)}, bf16[3,3,3,8,4]{3,4,2,1,0:T(4,128)(2,1)}, u32[]{:S(2)}) copy-start(bf16[3,3,3,8,4]{3,4,2,1,0:T(4,128)(2,1)} %param.14) | copy-start | bytes 5188
  20.5 160.4 %copy-start.14 = (u32[256]{0:T(256)S(1)}, u32[256]{0:T(256)}, u32[]{:S(2)}) copy-start(u32[256]{0:T(256)} %constant.108) | copy-start | bytes 3076
  170.3 0.6 copy-start.9
  172.2 16.9 %all-to-all-start = ((bf16[64,2,256]{2,1,0:T(2,128)(2,1)}), bf16[64,2,256]{2,1,0:T(2,128)(2,1)S(1)}, u32[]{:S(2)}, u32[]{:S(2)}) async-start(bf16[64,2,256]{2,1,0:T(2,128)(2,1)} %reshape.180), calls=%async_computation | async-start | bytes 131072 | tf_op jit(solution)/shard_map/all_to_all | solution.py:86
  198.1 26.0 %copy-start.10 = (f32[4]{0:T(128)S(1)}, f32[4]{0:T(128)}, u32[]{:S(2)}) copy-start(f32[4]{0:T(128)} %param.15) | copy-start | bytes 52
  198.1 26.1 %copy-start.12 = (f32[4]{0:T(128)S(1)}, f32[4]{0:T(128)}, u32[]{:S(2)}) copy-start(f32[4]{0:T(128)} %param.16) | copy-start | bytes 52
  198.1 26.9 %copy-start.4 = (bf16[1,4,64,2,32]{2,4,3,1,0:T(8,128)(2,1)S(1)}, bf16[1,4,64,2,32]{2,4,3,1,0:T(8,128)(2,1)}, u32[]{:S(2)}) copy-start(bf16[1,4,64,2,32]{2,4,3,1,0:T(8,128)(2,1)} %param.17) | copy-start | bytes 98308
  199.8 35.7 %copy-start.6 = (bf16[3,3,3,8,4]{3,4,2,1,0:T(4,128)(2,1)S(1)}, bf16[3,3,3,8,4]{3,4,2,1,0:T(4,128)(2,1)}, u32[]{:S(2)}) copy-start(bf16[3,3,3,8,4]{3,4,2,1,0:T(4,128)(2,1)} %rev.3) | copy-start | bytes 5188
  246.4 14.9 %all-to-all-start.1 = ((f32[64,1,512]{2,1,0:T(1,128)}), f32[64,1,512]{2,1,0:T(1,128)S(1)}, u32[]{:S(2)}, u32[]{:S(2)}) async-start(f32[64,1,512]{2,1,0:T(1,128)} %reshape.182), calls=%async_computation.1 | async-start | bytes 262144 | tf_op jit(solution)/shard_map/all_to_all | solution.py:144
  251.8 280.5 %all-reduce.10.cloned.1.call-start = ((), (), s32[]{:S(2)}) async-start(), calls=%async_computation.2 | async-start | bytes 7077888
  262.7 76.7 %copy-start.2 = (bf16[1,3,4,64,128]{4,0,3,2,1:T(2,128)(2,1)S(1)}, bf16[1,3,4,64,128]{4,0,3,2,1:T(2,128)(2,1)}, u32[]{:S(2)}) copy-start(bf16[1,3,4,64,128]{4,0,3,2,1:T(2,128)(2,1)} %copy-done.1) | copy-start | bytes 589828
  342.2 0.7 copy-start.13
  342.2 5.4 copy-start.3
Sparse Core Ops, SparseCore 0:
  342.4 189.9 all-reduce.9
where the time goes:
time: 568 us; the launch traced here: 559 us
  blocking collectives  259 us (46%)
  waiting for transfers between devices  173 us (30%)
  matrix products  45.4 us (8%)
  local copies, waits for them, and re-layouts  31 us (5%)
  between operations  16.8 us (3%)
  starting transfers between devices  15.5 us (3%)
  loops' own time  11.6 us (2%)
  other arithmetic  6.47 us (1%)
    unnamed x2, waiting for transfers between devices  151 us
    psum x1, blocking collectives, per_device(): lax.psum(jnp.sum(pre_one, axis=axes_last), ('dp', 'space')) / count  74.9 us
    psum x1, blocking collectives, per_device(): lax.psum(jnp.sum(jnp.square(pre_one - mean_one), axis=axes_last), ('dp',...  74.4 us
    psum x1, blocking collectives, per_device(): lax.psum((jnp.sum(grad_norm_one, axis=axes_last), jnp.sum(grad_norm_one *...  73.3 us
    conv_general_dilated x1, matrix products, group_filter(): lax.conv_general_dilated(inputs, grads, (1, 1, 1), ((1, 1), (1, 1), (1, 1...  29.6 us
    psum x1, blocking collectives, per_device(): summed = lax.psum(local_one, 'dp')  18.7 us
    another operation x1, loops' own time, combined_all(): lax.fori_loop(1, lax.axis_size(axis), lambda source, state: combine(state...  11.6 us
  transfers between devices with their start and end apart: 4, of which 4 were waited for; matrix products, arithmetic and copies ran while one was open for 7% of the time, Pallas kernels for 0%

commit v1 on v0

--- a/solution.py
+++ b/solution.py
@@ -67,7 +67,9 @@
     count = float(lax.axis_size("dp") * lead * planes * pre_one.shape[2] * pre_one.shape[3])
     axes_last = (0, 1, 2, 3)
     mean_one = lax.psum(jnp.sum(pre_one, axis=axes_last), ("dp", "space")) / count
-    spread_one = lax.psum(jnp.sum(jnp.square(pre_one - mean_one), axis=axes_last), ("dp", "space"))
+    part_2 = jnp.sum(jnp.square(pre_one - mean_one), axis=axes_last)
+    shards = lax.all_gather(part_2, ("dp", "space"))
+    spread_one = jnp.sum(shards, axis=0)
     var_one = spread_one / count
     inv_one = lax.rsqrt(var_one + EPS)
     norm_one = (pre_one - mean_one) * inv_one

time: 568 us -> 551 us (0.970)
  blocking collectives: 259 us -> 244 us
    psum x1 -> x0, blocking collectives: 74.4 us -> none  [per_device(): lax.psum(jnp.sum(jnp.square(pre_one - mean_one), axis=axes_last), ('dp',...]
    all_gather x0 -> x1, blocking collectives: none -> 59.6 us  [per_device(): shards = lax.all_gather(part_2, ('dp', 'space'))]
  transfers between devices with their start and end apart: 4 -> 4, of which waited for: 4 -> 4; matrix products, arithmetic and copies ran while one was open for 7% -> 8% of each run, Pallas kernels for 0% -> 0%
where the time goes in v1:
time: 551 us; the launch traced here: 542 us
  blocking collectives  244 us (44%)
  waiting for transfers between devices  173 us (31%)
  matrix products  45.3 us (8%)
  local copies, waits for them, and re-layouts  28.8 us (5%)
  between operations  16.6 us (3%)
  starting transfers between devices  16 us (3%)
  loops' own time  10.6 us (2%)
  other arithmetic  6.7 us (1%)
    unnamed x2, waiting for transfers between devices  151 us
    psum x1, blocking collectives, per_device(): lax.psum(jnp.sum(pre_one, axis=axes_last), ('dp', 'space')) / count  74.9 us
    psum x1, blocking collectives, per_device(): lax.psum((jnp.sum(grad_norm_one, axis=axes_last), jnp.sum(grad_norm_one *...  73.6 us
    all_gather x1, blocking collectives, per_device(): shards = lax.all_gather(part_2, ('dp', 'space'))  59.6 us
    conv_general_dilated x1, matrix products, group_filter(): lax.conv_general_dilated(inputs, grads, (1, 1, 1), ((1, 1), (1, 1), (1, 1...  29.6 us
    psum x1, blocking collectives, per_device(): summed = lax.psum(local_one, 'dp')  18.7 us
  transfers between devices with their start and end apart: 4, of which 4 were waited for; matrix products, arithmetic and copies ran while one was open for 8% of the time, Pallas kernels for 0%

profile of v1, /device:TPU:2, one launch (start us, length us, event | category | flops | bytes accessed | tf_op | source)
XLA Modules:
  0.0 542.0 jit_solution(12251253862458468227)
XLA Ops:
  7.2 1.0 slice.21
  8.3 1.9 collective-permute-start
  10.2 7.9 %collective-permute-done = bf16[1,1,4,64,128]{4,0,3,2,1:T(2,128)(2,1)S(1)} collective-permute-done((bf16[1,1,4,64,128]{4,0,3,2,1:T(2,128)(2,1)S(1)}, bf16[1,1,4,64,128]{4,0,3,2,1:T(2,128)(2,1)S(1)}, u32[]{:S(2)}, u32[]{:S(2)}) %collective-permute-start) | collective-permute-done | bytes 65568 | tf_op jit(solution)/shard_map/ppermute | solution.py:15
  18.1 0.1 constant_dynamic-update-slice_fusion.1
  18.2 1.1 constant_dynamic-update-slice_fusion
  19.4 0.7 copy-done.1
  20.2 0.2 copy.244
  20.5 0.4 select_reduce_fusion.3
  21.0 74.9 %psum.49 = f32[256]{0:T(256)S(1)} all-reduce(f32[256]{0:T(256)S(1)} %get-tuple-element.289), channel_id=1, replica_groups=mesh['dp'=4,'space'=64] {'dp','space'}, use_global_device_ids=true, to_apply=%region_1.0 | all-reduce | flops 256 | bytes 2048 | tf_op jit(solution)/shard_map/psum | solution.py:69
  96.0 59.6 %all-gather.3 = f32[256,1,256]{2,1,0:T(1,128)S(1)} all-gather(f32[1,1,256]{2,1,0:T(1,128)S(1)} %bitcast.177), channel_id=2, replica_groups=mesh['dp'=4,'space'=64] {'dp','space'}, dimensions={0}, use_global_device_ids=true | all-gather | bytes 263168 | tf_op jit(solution)/shard_map/all_gather | solution.py:71
  155.6 0.3 reduce_sum.92
  155.9 0.7 add_multiply_fusion
  156.8 0.1 copy.203
  157.0 0.1 broadcast_in_dim.11
  157.1 0.8 reshape.188
  157.9 8.5 %all-to-all-start = ((bf16[64,2,256]{2,1,0:T(2,128)(2,1)}), bf16[64,2,256]{2,1,0:T(2,128)(2,1)S(1)}, u32[]{:S(2)}, u32[]{:S(2)}) async-start(bf16[64,2,256]{2,1,0:T(2,128)(2,1)} %reshape.188), calls=%async_computation | async-start | bytes 131072 | tf_op jit(solution)/shard_map/all_to_all | solution.py:88
  166.5 0.6 rev.3
  167.1 0.6 dynamic-slice
  168.3 0.7 dynamic-update-slice
  169.1 6.2 %all-to-all-done = bf16[64,2,256]{2,1,0:T(2,128)(2,1)S(1)} async-done(((bf16[64,2,256]{2,1,0:T(2,128)(2,1)}), bf16[64,2,256]{2,1,0:T(2,128)(2,1)S(1)}, u32[]{:S(2)}, u32[]{:S(2)}) %all-to-all-start) | async-done | bytes 65568 | tf_op jit(solution)/shard_map/all_to_all | solution.py:88
  175.3 0.2 reshape.189
  175.5 0.2 copy.245
  175.8 1.0 copy.207
  176.8 0.2 slice.24
  177.0 5.6 %fusion.8 = f32[64,2,8,5,4]{2,4,3,1,0:T(4,128)} fusion(bf16[3,3,3,8,4]{3,4,2,1,0:T(4,128)(2,1)S(1)} %copy-done.8, bf16[8,64,2,1,7,2]{4,0,5,2,1,3:T(8,128)(2,1)S(1)} %slice.24, bf16[8,64,2,1,8,5]{4,0,5,2,1,3:T(8,128)(2,1)S(1)} %copy.207), kind=kOutput, calls=%fused_computation.13 | convolution fusion | flops 6180864 | bytes 194240 | tf_op jit(solution)/shard_map/conv_general_dilated | solution.py:92
  182.6 1.7 copy.208
  184.3 0.2 select_reduce_fusion.1
  184.6 0.2 select_reduce_fusion
  184.8 0.2 dynamic-update-slice.2
  185.0 9.7 %all-reduce.7 = (f32[4]{0:T(128)S(1)}, f32[16]{0:T(128)S(1)}, f32[16]{0:T(128)S(1)}) all-reduce(f32[4]{0:T(128)S(1)} %dynamic-update-slice, f32[16]{0:T(128)S(1)} %get-tuple-element.288, f32[16]{0:T(128)S(1)} %dynamic-update-slice.2), channel_id=1, replica_groups=mesh['dp'=4,'space'=64] {'dp'}, use_global_device_ids=true, to_apply=%add | all-reduce | flops 36 | bytes 288
  195.4 12.4 %while.19 = (s32[]{:T(128)}, f32[1,1,1,1,1]{4,3,2,1,0:T(1,128)}, f32[1,4,1,1,1]{1,4,3,2,0:T(1,128)S(1)}, f32[1,4,1,1,1]{1,4,3,2,0:T(1,128)S(1)}, f32[4,1,1,1,1,1...) while((s32[]{:T(128)}, f32[1,1,1,1,1]{4,3,2,1,0:T(1,128)}, ...), condition=%wide.region_7.8_spmd, body=%wide.region_6.7_spmd.sunk | while | flops 37 | bytes 303 | solution.py:24
  195.4 0.6 constant_dynamic-slice_fusion.5
  199.5 0.6 constant_dynamic-slice_fusion.5
  203.7 0.6 constant_dynamic-slice_fusion.5
  207.8 0.7 rsqrt_bitcast_fusion
  208.5 0.8 add_convert_fusion
  209.3 0.3 fusion.39
  209.6 8.0 %all-reduce.6 = (f32[1,4,1,1,1]{1,4,3,2,0:T(1,128)S(1)}, f32[1,4,1,1,1]{1,4,3,2,0:T(1,128)S(1)}) all-reduce(f32[1,4,1,1,1]{1,4,3,2,0:T(1,128)S(1)} %bitcast.179, f32[1,4,1,1,1]{1,4,3,2,0:T(1,128)S(1)} %bitcast.178), channel_id=1, replica_groups=mesh['dp'=4,'space'=64] {'dp'}, use_global_device_ids=true, to_apply=%region_11.12 | all-reduce | flops 8 | bytes 64 | tf_op jit(solution)/shard_map/psum | solution.py:116
  217.9 0.4 copy.218
  218.3 0.2 slice.28
  218.5 6.9 %convolution_select_fusion = f32[64,2,8,5,8]{4,2,3,1,0:T(8,128)} fusion(pred[8,5]{0,1:T(8,128)(4,1)S(1)} %copy-done.10, bf16[4,64,2,1,7,2]{4,0,5,2,1,3:T(4,128)(2,1)S(1)} %slice.28, bf16[4,64,2,1,8,5]{4,0,5,2,1,3:T(4,128)(2,1)S(1)} %copy.218, bf16[3,3,3,8,4]{3,4,2,1,0:T(4,128)(2,1)S(1)} %copy-done.9), kind=kOutput, calls=%fused_computation.19 | convolution fusion | flops 6049792 | bytes 220904 | tf_op jit(solution)/shard_map/conv_general_dilated | solution.py:137
  225.4 2.7 copy.219
  228.1 0.3 copy.220
  228.4 0.9 reshape.190
  229.3 5.5 %all-to-all-start.1 = ((f32[64,1,512]{2,1,0:T(1,128)}), f32[64,1,512]{2,1,0:T(1,128)S(1)}, u32[]{:S(2)}, u32[]{:S(2)}) async-start(f32[64,1,512]{2,1,0:T(1,128)} %reshape.190), calls=%async_computation.1 | async-start | bytes 262144 | tf_op jit(solution)/shard_map/all_to_all | solution.py:146
  235.2 0.8 copy.241
  236.0 8.2 %all-to-all-done.1 = f32[64,1,512]{2,1,0:T(1,128)S(1)} async-done(((f32[64,1,512]{2,1,0:T(1,128)}), f32[64,1,512]{2,1,0:T(1,128)S(1)}, u32[]{:S(2)}, u32[]{:S(2)}) %all-to-all-start.1) | async-done | bytes 131104 | tf_op jit(solution)/shard_map/all_to_all | solution.py:146
  244.2 0.5 broadcast.193
  244.7 0.9 reduce.2
  245.7 0.2 reshape.191
  245.9 0.7 reduce_sum.97
  246.6 1.3 fusion.51
  247.9 73.6 %all-reduce.4 = (f32[256]{0:T(256)S(1)}, f32[256]{0:T(256)S(1)}) all-reduce(f32[256]{0:T(256)S(1)} %get-tuple-element.252, f32[256]{0:T(256)S(1)} %get-tuple-element.251), channel_id=1, replica_groups=mesh['dp'=4,'space'=64] {'dp','space'}, use_global_device_ids=true, to_apply=%region_16.17 | all-reduce | flops 512 | bytes 4096 | tf_op jit(solution)/shard_map/psum | solution.py:153
  321.8 0.1 fusion.31
  322.0 2.8 fusion.53
  324.9 0.6 copy-done.15
  325.6 0.6 dynamic-slice.3
  326.8 3.5 copy.231
  330.3 0.6 copy.232
  331.0 3.6 copy.230
  334.6 29.6 %fusion.54 = f32[3,3,3,8,4]{3,4,2,1,0:T(4,128)S(1)} fusion(bf16[1,8,64,2,32]{1,0,4,3,2:T(2,128)(2,1)} %copy.230, bf16[1,4,64,2,32]{1,0,4,3,2:T(2,128)(2,1)} %copy.231), kind=kOutput, calls=%fused_computation.97 | convolution fusion | flops 4572160 | bytes 101760 | tf_op jit(solution)/shard_map/vmap()/conv_general_dilated | solution.py:42
  364.2 151.2 %all-reduce.10.cloned.1.call-done = f32[3,3,3,128,256]{3,4,2,1,0:T(8,128)} async-done(((f32[3,3,3,128,256]{3,4,2,1,0:T(8,128)}), f32[3,3,3,128,256]{3,4,2,1,0:T(8,128)}) %all-reduce.10.cloned.1.call-update) | async-done | bytes 3538960
  515.3 0.9 constant_dynamic-slice_fusion.3
  516.2 18.7 %all-reduce.5 = (f32[3,3,3,128,4]{3,4,2,1,0:T(4,128)}, f32[3,3,3,8,4]{3,4,2,1,0:T(4,128)}) all-reduce(f32[3,3,3,128,4]{3,4,2,1,0:T(4,128)S(1)} %constant_dynamic-slice_fusion.3, f32[3,3,3,8,4]{3,4,2,1,0:T(4,128)S(1)} %fusion.54), channel_id=1, replica_groups=mesh['dp'=4,'space'=64] {'dp'}, use_global_device_ids=true, to_apply=%region_17.18 | all-reduce | flops 14688 | bytes 117504 | tf_op jit(solution)/shard_map/psum | solution.py:169
  (80 shorter events, 2.1 us)
Async XLA Ops:
  7.2 13.3 %copy-start = (bf16[3,3,3,128,256]{4,3,2,1,0:T(8,128)(2,1)S(1)}, bf16[3,3,3,128,256]{4,3,2,1,0:T(8,128)(2,1)}, u32[]{:S(2)}) copy-start(bf16[3,3,3,128,256]{4,3,2,1,0:T(8,128)(2,1)} %param.11) | copy-start | bytes 5308420
  7.2 13.3 %copy-start.10 = (pred[8,5]{0,1:T(8,128)(4,1)S(1)}, pred[8,5]{0,1:T(8,128)(4,1)}, u32[]{:S(2)}) copy-start(pred[8,5]{0,1:T(8,128)(4,1)} %constant.99) | copy-start | bytes 124
  8.3 9.8 %collective-permute-start = (bf16[1,1,4,64,128]{4,0,3,2,1:T(2,128)(2,1)S(1)}, bf16[1,1,4,64,128]{4,0,3,2,1:T(2,128)(2,1)S(1)}, u32[]{:S(2)}, u32[]{:S(2)}) collective-permute-start(bf16[1,1,4,64,128]{4,0,3,2,1:T(2,128)(2,1)S(1)} %copy.254), channel_id=1, source_target_pairs={{0,1},{1,2},{2,3},{3,4},{4,5},{5,6},{6,7},{7,8},{8,9},{9,10},{10,1... | collective-permute-start | bytes 196616 | tf_op jit(solution)/shard_map/ppermute | solution.py:15
  19.4 0.7 copy-start.1
  20.2 135.7 %copy-start.11 = (f32[256]{0:T(256)S(1)}, f32[256]{0:T(256)}, u32[]{:S(2)}) copy-start(f32[256]{0:T(256)} %param.12) | copy-start | bytes 3076
  20.2 135.7 %copy-start.13 = (f32[256]{0:T(256)S(1)}, f32[256]{0:T(256)}, u32[]{:S(2)}) copy-start(f32[256]{0:T(256)} %param.13) | copy-start | bytes 3076
  20.5 145.9 %copy-start.8 = (bf16[3,3,3,8,4]{3,4,2,1,0:T(4,128)(2,1)S(1)}, bf16[3,3,3,8,4]{3,4,2,1,0:T(4,128)(2,1)}, u32[]{:S(2)}) copy-start(bf16[3,3,3,8,4]{3,4,2,1,0:T(4,128)(2,1)} %param.14) | copy-start | bytes 5188
  20.5 146.6 %copy-start.16 = (u32[256]{0:T(256)S(1)}, u32[256]{0:T(256)}, u32[]{:S(2)}) copy-start(u32[256]{0:T(256)} %constant.108) | copy-start | bytes 3076
  156.6 18.9 %copy-start.3 = (f32[1,2,8,5,256]{4,2,3,1,0:T(8,128)}, f32[1,2,8,5,256]{4,2,3,1,0:T(8,128)S(1)}, u32[]{:S(2)}) copy-start(f32[1,2,8,5,256]{4,2,3,1,0:T(8,128)S(1)} %get-tuple-element.280) | copy-start | bytes 245764
  157.9 17.3 %all-to-all-start = ((bf16[64,2,256]{2,1,0:T(2,128)(2,1)}), bf16[64,2,256]{2,1,0:T(2,128)(2,1)S(1)}, u32[]{:S(2)}, u32[]{:S(2)}) async-start(bf16[64,2,256]{2,1,0:T(2,128)(2,1)} %reshape.188), calls=%async_computation | async-start | bytes 131072 | tf_op jit(solution)/shard_map/all_to_all | solution.py:88
  182.6 25.9 %copy-start.12 = (f32[4]{0:T(128)S(1)}, f32[4]{0:T(128)}, u32[]{:S(2)}) copy-start(f32[4]{0:T(128)} %param.15) | copy-start | bytes 52
  182.6 25.9 %copy-start.14 = (f32[4]{0:T(128)S(1)}, f32[4]{0:T(128)}, u32[]{:S(2)}) copy-start(f32[4]{0:T(128)} %param.16) | copy-start | bytes 52
  182.6 26.7 %copy-start.7 = (bf16[1,4,64,2,32]{2,4,3,1,0:T(8,128)(2,1)S(1)}, bf16[1,4,64,2,32]{2,4,3,1,0:T(8,128)(2,1)}, u32[]{:S(2)}) copy-start(bf16[1,4,64,2,32]{2,4,3,1,0:T(8,128)(2,1)} %param.17) | copy-start | bytes 98308
  184.3 34.2 %copy-start.9 = (bf16[3,3,3,8,4]{3,4,2,1,0:T(4,128)(2,1)S(1)}, bf16[3,3,3,8,4]{3,4,2,1,0:T(4,128)(2,1)}, u32[]{:S(2)}) copy-start(bf16[3,3,3,8,4]{3,4,2,1,0:T(4,128)(2,1)} %rev.3) | copy-start | bytes 5188
  225.4 9.5 %copy-start.4 = (f32[1,2,8,5,256]{4,2,3,1,0:T(8,128)S(1)}, f32[1,2,8,5,256]{4,2,3,1,0:T(8,128)}, u32[]{:S(2)}) copy-start(f32[1,2,8,5,256]{4,2,3,1,0:T(8,128)} %copy-done.3) | copy-start | bytes 245764
  225.4 9.5 %copy-start.5 = (f32[1,2,8,5,256]{4,2,3,1,0:T(8,128)S(1)}, f32[1,2,8,5,256]{4,2,3,1,0:T(8,128)}, u32[]{:S(2)}) copy-start(f32[1,2,8,5,256]{4,2,3,1,0:T(8,128)} %get-tuple-element.279) | copy-start | bytes 245764
  229.3 14.9 %all-to-all-start.1 = ((f32[64,1,512]{2,1,0:T(1,128)}), f32[64,1,512]{2,1,0:T(1,128)S(1)}, u32[]{:S(2)}, u32[]{:S(2)}) async-start(f32[64,1,512]{2,1,0:T(1,128)} %reshape.190), calls=%async_computation.1 | async-start | bytes 262144 | tf_op jit(solution)/shard_map/all_to_all | solution.py:146
  234.8 280.5 %all-reduce.10.cloned.1.call-start = ((), (), s32[]{:S(2)}) async-start(), calls=%async_computation.2 | async-start | bytes 7077888
  245.7 76.3 %copy-start.2 = (bf16[1,3,4,64,128]{4,0,3,2,1:T(2,128)(2,1)S(1)}, bf16[1,3,4,64,128]{4,0,3,2,1:T(2,128)(2,1)}, u32[]{:S(2)}) copy-start(bf16[1,3,4,64,128]{4,0,3,2,1:T(2,128)(2,1)} %copy-done.1) | copy-start | bytes 589828
  324.9 0.7 copy-start.15
  324.9 5.4 copy-start.6
Sparse Core Ops, SparseCore 0:
  325.0 190.2 all-reduce.9
